TPU v7x, 32 devices: a whole 2x2x4 slice. The times are simulated.
32 devices in a mesh: pts: 8 (over y, x, core), val: 4 (over z).
Axes of the slice: x: 2, y: 2, z: 4, core: 2. Of those that a mesh axis runs over, the one named last changes fastest.
Arguments:
- trials: bfloat16 [2, 1024, 1024], P(None, 'val', 'pts'), may hold values from -6 to 6
- psi_val: bfloat16 [8192, 1024], P('pts', 'val'), may hold values from -0.1875 to 0.1875
- psi_cond: bfloat16 [8192, 1024], P('pts'), may hold values from -0.1875 to 0.1875
- kernel: bfloat16 [8192, 8192], P(None, ('pts', 'val')), may hold values from -0.5 to 0.5
- eps_val: float32 [1024], P('val'), may hold values from -1.75 to -0.25
- eps_cond: float32 [1024], replicated, may hold values from 0.5 to 1.5
Outputs:
- first: float32 [2, 1024, 1024], P(None, 'val', 'pts')
- filtered: float32 [2, 1024, 1024], P(None, 'val', 'pts')
All inputs are finite; a program needn't handle non-finite values.
Results may differ from a plain program's by a relative error of at most 0.025.
Values may be sent and summed in bfloat16 or wider, within the bound.
A program may use at most 64 MiB of HBM per device.

v0:
```python
import jax
import jax.numpy as jnp
from jax import lax
from jax.sharding import PartitionSpec as P

center_shift = 1.75
half_width = 1.25


def gathered_inner(local_trial, psi_cond):
    return jnp.einsum(
        "kvc,mc->kvm",
        lax.all_gather(local_trial, "pts", axis=2, tiled=True),
        psi_cond,
        preferred_element_type=jnp.float32,
    )


def orbital_terms(inner, psi_val, psi_cond, kernel):
    rho_part = jnp.einsum("mv,kvm->km", psi_val.astype(jnp.float32), inner)
    rho = lax.psum_scatter(rho_part, "val", scatter_dimension=1, tiled=True).astype(jnp.bfloat16)
    image_part = jnp.einsum("km,nm->kn", rho, kernel, preferred_element_type=jnp.float32)
    image_rows = lax.psum_scatter(
        image_part.astype(jnp.bfloat16), "pts", scatter_dimension=1, tiled=True
    ).astype(jnp.float32)
    image = lax.psum(image_rows, "val")
    weighted = (jnp.transpose(psi_val.astype(jnp.float32))[None] * image[:, None, :]).astype(
        jnp.bfloat16
    )
    return jnp.einsum("kvm,mc->kvc", weighted, psi_cond, preferred_element_type=jnp.float32)


def reduced(partial_sum):
    return lax.psum_scatter(
        partial_sum.astype(jnp.bfloat16), "pts", scatter_dimension=2, tiled=True
    ).astype(jnp.float32)


def local(trials, psi_val, psi_cond, kernel, eps_val, eps_cond):
    cols_own = trials.shape[2]
    index_pts = lax.axis_index("pts")
    diff_whole = (eps_cond[None, :] - eps_val[:, None] - center_shift)[None]
    diff_own = lax.dynamic_slice_in_dim(diff_whole, index_pts * cols_own, cols_own, 2)
    first_image = reduced(
        orbital_terms(gathered_inner(trials, psi_cond), psi_val, psi_cond, kernel)
    )
    first = (diff_own * trials.astype(jnp.float32) + 2.0 * first_image) / half_width
    second_trial = first.astype(jnp.bfloat16)
    second_inner = gathered_inner(second_trial, psi_cond)
    second_image = reduced(orbital_terms(second_inner, psi_val, psi_cond, kernel))
    filtered = 2.0 * (
        diff_own * second_trial.astype(jnp.float32) + 2.0 * second_image
    ) / half_width - trials.astype(jnp.float32)
    return (first, filtered)


def solution(mesh):
    in_specs = (
        P(None, "val", "pts"),
        P("pts", "val"),
        P("pts", None),
        P(None, ("pts", "val")),
        P("val"),
        P(),
    )
    out_specs = (P(None, "val", "pts"), P(None, "val", "pts"))
    return jax.shard_map(local, mesh=mesh, in_specs=in_specs, out_specs=out_specs, check_vma=False)
```

profile of v0, /device:TPU:0, one launch (start us, length us, event | category | flops | bytes accessed | tf_op | source)
XLA Modules:
  0.0 326.2 jit_solution(14909899464436743166)
XLA Ops:
  7.2 0.0 all-gather.3.cloned.1.call-start
  7.2 0.7 all-gather.3.cloned.1.call-update
  7.9 0.0 reduce-scatter.15.cloned.1.call-start
  8.0 28.1 %all-gather.3.cloned.1.call-done = bf16[2,256,1024]{2,1,0:T(8,128)(2,1)} async-done(((bf16[2,256,128]{2,1,0:T(8,128)(2,1)}), bf16[2,256,1024]{2,1,0:T(8,128)(2,1)}) %all-gather.3.cloned.1.call-update) | async-done | bytes 1048592 | tf_op jit(solution)/shard_map/all_gather | solution.py:13
  36.1 2.5 fusion.6
  38.6 2.0 copy.10
  40.6 3.4 %fusion.20 = f32[1024,1,2]{2,1,0:T(1,128)} fusion(bf16[2,256,1024]{1,0,2:T(2,128)(2,1)} %copy.10, bf16[1024,256,1]{1,0,2:T(8,128)(2,1)} %bitcast.48), kind=kOutput, calls=%fused_computation.21 | convolution fusion | flops 1048576 | bytes 1581056 | tf_op jit(solution)/shard_map/mv,kvm->km/dot_general | solution.py:20
  44.0 0.0 reduce-scatter.15.cloned.1.call-update
  44.1 0.0 reduce-scatter.19.cloned.1.call-start
  44.1 22.0 %reduce-scatter.15.cloned.1.call-done = f32[2,256]{0,1:T(8,128)} async-done(((f32[2,1024]{0,1:T(8,128)}), f32[2,256]{0,1:T(8,128)}) %reduce-scatter.15.cloned.1.call-update) | async-done | bytes 2064 | tf_op jit(solution)/shard_map/reduce_scatter | solution.py:21
  66.1 3.4 %convolution_convert_fusion.1 = bf16[2,8192]{1,0:T(2,128)(2,1)S(1)} fusion(bf16[8192,256]{1,0:T(8,128)(2,1)} %param.9, f32[2,256]{0,1:T(8,128)} %reduce-scatter.15.cloned.1.call-done), kind=kOutput, calls=%fused_computation.1 | convolution fusion | flops 8405504 | bytes 4229120 | tf_op jit(solution)/shard_map/km,nm->kn/dot_general | solution.py:22
  69.5 1.9 copy.15
  71.4 0.0 reduce-scatter.21.cloned.1.call-start
  71.5 1.1 convert_bitcast_fusion
  72.6 1.3 copy.9
  74.0 37.0 %reduce-scatter.19.cloned.1.call-done = bf16[1024,2]{1,0:T(8,128)(2,1)} async-done(((bf16[8192,2]{1,0:T(8,128)(2,1)}), bf16[1024,2]{1,0:T(8,128)(2,1)}) %reduce-scatter.19.cloned.1.call-update) | async-done | bytes 4112
  111.0 1.1 copy.16
  112.0 11.9 %psum.14 = f32[2,1024]{1,0:T(2,128)S(1)} all-reduce(bf16[2,1024]{1,0:T(2,128)(2,1)S(1)} %copy.16), channel_id=1, replica_groups=mesh['pts'=8,'val'=4] {'val'}, use_global_device_ids=true, to_apply=%region_2.0 | all-reduce | flops 2048 | bytes 12288 | tf_op jit(solution)/shard_map/psum | solution.py:26
  124.0 3.4 %fusion.8 = bf16[2,256,1024]{2,1,0:T(8,128)(2,1)} fusion(bf16[1024,1024]{1,0:T(8,128)(2,1)S(1)} %copy-done, f32[2,1024]{1,0:T(2,128)S(1)} %psum.14, f32[256,1024]{1,0:T(8,128)} %copy.9), kind=kOutput, calls=%fused_computation.12 | convolution fusion | flops 1075314688 | bytes 4202496 | tf_op jit(solution)/shard_map/kvm,mc->kvc/dot_general | solution.py:30
  127.4 2.5 copy.17
  130.0 1.2 copy.23
  131.2 0.0 all-gather.5.cloned.1.call-start
  131.2 0.8 dynamic-slice.4
  132.0 0.1 subtract_add_fusion
  132.1 32.4 %reduce-scatter.21.cloned.1.call-done = bf16[128,512]{1,0:T(8,128)(2,1)} async-done(((bf16[1024,512]{1,0:T(8,128)(2,1)}), bf16[128,512]{1,0:T(8,128)(2,1)}) %reduce-scatter.21.cloned.1.call-update) | async-done | bytes 131088
  164.5 0.9 reshape.18
  165.5 0.1 copy.18
  165.6 0.8 fusion.26
  166.4 0.0 reduce-scatter.17.cloned.1.call-start
  166.5 23.8 %all-gather.5.cloned.1.call-done = bf16[2,256,1024]{2,1,0:T(8,128)(2,1)} async-done(((bf16[2,256,128]{2,1,0:T(8,128)(2,1)}), bf16[2,256,1024]{2,1,0:T(8,128)(2,1)}) %all-gather.5.cloned.1.call-update) | async-done | bytes 1048592 | tf_op jit(solution)/shard_map/all_gather | solution.py:13
  190.3 2.5 fusion.2
  192.9 2.0 copy.13
  194.9 3.4 %fusion.18 = f32[1024,1,2]{2,1,0:T(1,128)} fusion(bf16[2,256,1024]{1,0,2:T(2,128)(2,1)} %copy.13, bf16[1024,256,1]{1,0,2:T(8,128)(2,1)} %bitcast.49), kind=kOutput, calls=%fused_computation.19 | convolution fusion | flops 1048576 | bytes 1581056 | tf_op jit(solution)/shard_map/mv,kvm->km/dot_general | solution.py:20
  198.3 0.0 reduce-scatter.23.cloned.1.call-start
  198.3 22.0 %reduce-scatter.17.cloned.1.call-done = f32[2,256]{0,1:T(8,128)} async-done(((f32[2,1024]{0,1:T(8,128)}), f32[2,256]{0,1:T(8,128)}) %reduce-scatter.17.cloned.1.call-update) | async-done | bytes 2064 | tf_op jit(solution)/shard_map/reduce_scatter | solution.py:21
  220.3 3.4 %convolution_convert_fusion = bf16[2,8192]{1,0:T(2,128)(2,1)S(1)} fusion(bf16[8192,256]{1,0:T(8,128)(2,1)} %param.9, f32[2,256]{0,1:T(8,128)} %reduce-scatter.17.cloned.1.call-done), kind=kOutput, calls=%fused_computation | convolution fusion | flops 8405504 | bytes 4229120 | tf_op jit(solution)/shard_map/km,nm->kn/dot_general | solution.py:22
  223.7 1.9 copy.19
  225.7 0.0 reduce-scatter.25.cloned.1.call-start
  225.7 39.5 %reduce-scatter.23.cloned.1.call-done = bf16[1024,2]{1,0:T(8,128)(2,1)} async-done(((bf16[8192,2]{1,0:T(8,128)(2,1)}), bf16[1024,2]{1,0:T(8,128)(2,1)}) %reduce-scatter.23.cloned.1.call-update) | async-done | bytes 4112
  265.2 1.1 copy.20
  266.3 11.9 %psum.15 = f32[2,1024]{1,0:T(2,128)S(1)} all-reduce(bf16[2,1024]{1,0:T(2,128)(2,1)S(1)} %copy.20), channel_id=1, replica_groups=mesh['pts'=8,'val'=4] {'val'}, use_global_device_ids=true, to_apply=%region_6.0 | all-reduce | flops 2048 | bytes 12288 | tf_op jit(solution)/shard_map/psum | solution.py:26
  278.2 2.2 fusion.11
  280.4 2.5 copy.21
  283.0 1.2 copy.24
  284.2 33.3 %reduce-scatter.25.cloned.1.call-done = bf16[128,512]{1,0:T(8,128)(2,1)} async-done(((bf16[1024,512]{1,0:T(8,128)(2,1)}), bf16[128,512]{1,0:T(8,128)(2,1)}) %reduce-scatter.25.cloned.1.call-update) | async-done | bytes 131088
  317.5 0.9 reshape.22
  318.5 0.1 copy.22
  318.6 0.8 convert_subtract_fusion
  (16 shorter events, 0.1 us)
Async XLA Ops:
  7.2 28.9 %copy-start = (bf16[1024,1024]{1,0:T(8,128)(2,1)S(1)}, bf16[1024,1024]{1,0:T(8,128)(2,1)}, u32[]{:S(2)}) copy-start(bf16[1024,1024]{1,0:T(8,128)(2,1)} %param.8) | copy-start | bytes 6291460
  7.2 28.9 %all-gather.3.cloned.1.call-start = ((), (), s32[]{:S(2)}) async-start(), calls=%async_computation.6 | async-start | bytes 1179648 | tf_op jit(solution)/shard_map/all_gather | solution.py:13
  7.9 58.2 %reduce-scatter.15.cloned.1.call-start = ((), (), s32[]{:S(2)}) async-start(), calls=%async_computation.7 | async-start | bytes 655360 | tf_op jit(solution)/shard_map/reduce_scatter | solution.py:21
  44.1 66.9 %reduce-scatter.19.cloned.1.call-start = ((), (), s32[]{:S(2)}) async-start(), calls=%async_computation.10 | async-start | bytes 2359296
  71.4 93.1 %reduce-scatter.21.cloned.1.call-start = ((), (), s32[]{:S(2)}) async-start(), calls=%async_computation.11 | async-start | bytes 1179648
  129.9 2.1 copy-start.4
  129.9 35.7 %copy-start.1 = (bf16[2,256,128]{2,1,0:T(8,128)(2,1)S(1)}, bf16[2,256,128]{2,1,0:T(8,128)(2,1)}, u32[]{:S(2)}) copy-start(bf16[2,256,128]{2,1,0:T(8,128)(2,1)} %param.6) | copy-start | bytes 393220
  131.2 59.2 %all-gather.5.cloned.1.call-start = ((), (), s32[]{:S(2)}) async-start(), calls=%async_computation.8 | async-start | bytes 1179648 | tf_op jit(solution)/shard_map/all_gather | solution.py:13
  166.4 53.9 %reduce-scatter.17.cloned.1.call-start = ((), (), s32[]{:S(2)}) async-start(), calls=%async_computation.9 | async-start | bytes 655360 | tf_op jit(solution)/shard_map/reduce_scatter | solution.py:21
  198.3 66.9 %reduce-scatter.23.cloned.1.call-start = ((), (), s32[]{:S(2)}) async-start(), calls=%async_computation.12 | async-start | bytes 2359296
  223.7 54.5 %copy-start.3 = (f32[256,1024]{1,0:T(8,128)S(1)}, f32[256,1024]{1,0:T(8,128)}, u32[]{:S(2)}) copy-start(f32[256,1024]{1,0:T(8,128)} %copy.9) | copy-start | bytes 3145732
  225.7 91.9 %reduce-scatter.25.cloned.1.call-start = ((), (), s32[]{:S(2)}) async-start(), calls=%async_computation.13 | async-start | bytes 1179648
  283.0 35.7 %copy-start.2 = (bf16[2,256,128]{2,1,0:T(8,128)(2,1)S(1)}, bf16[2,256,128]{2,1,0:T(8,128)(2,1)}, u32[]{:S(2)}) copy-start(bf16[2,256,128]{2,1,0:T(8,128)(2,1)} %get-tuple-element.2) | copy-start | bytes 393220
Sparse Core Ops, SparseCore 0:
  9.9 26.1 all-gather.2
  44.2 21.8 reduce-scatter.14
  71.6 39.3 reduce-scatter.18
  131.3 33.1 reduce-scatter.20
  166.8 23.4 all-gather.4
  198.4 21.8 reduce-scatter.16
  225.8 39.3 reduce-scatter.22
  284.3 33.1 reduce-scatter.24
where the time goes:
time: 327 us; the launch traced here: 326 us
  waiting for transfers between devices  239 us (73%)
  matrix products  24.3 us (7%)
  blocking collectives  23.8 us (7%)
  local copies, waits for them, and re-layouts  21.7 us (7%)
  between operations  14.3 us (4%)
    unnamed x12, waiting for transfers between devices  143 us
    all_gather x2, waiting for transfers between devices, gathered_inner(): lax.all_gather(local_trial, 'pts', axis=2, tiled=True)  52 us
    reduce_scatter x2, waiting for transfers between devices, orbital_terms(): lax.psum_scatter(rho_part, 'val', scatter_dimension=1, tiled=True)  43.9 us
    psum x2, blocking collectives, orbital_terms(): image = lax.psum(image_rows, 'val')  23.8 us
    unnamed x22, local copies, waits for them, and re-layouts  15.6 us
    dot_general x2, matrix products, orbital_terms(): jnp.einsum('km,nm->kn', rho, kernel, preferred_element_type=jnp.float32)  6.88 us
    dot_general x2, matrix products, orbital_terms(): rho_part = jnp.einsum('mv,kvm->km', psi_val.astype(jnp.float32), inner)  6.78 us
  transfers between devices with their start and end apart: 8, of which 8 were waited for; matrix products, arithmetic and copies ran while one was open for 1% of the time, Pallas kernels for 0%

commit v1 on v0

--- a/solution.py
+++ b/solution.py
@@ -8,9 +8,14 @@
 
 
 def gathered_inner(local_trial, psi_cond):
+
+    def raise_sites(arr_in, which_axis):
+        response = jnp.concatenate([arr_in] * jax.lax.axis_size(which_axis), 2)
+        return jax.lax.all_to_all(response, which_axis, 2, 2, tiled=True)
+
     return jnp.einsum(
         "kvc,mc->kvm",
-        lax.all_gather(local_trial, "pts", axis=2, tiled=True),
+        raise_sites(local_trial, which_axis="pts"),
         psi_cond,
         preferred_element_type=jnp.float32,
     )

time: 327 us -> 333 us (1.018)
  waiting for transfers between devices: 239 us -> 185 us
  blocking collectives: 23.8 us -> 62.1 us
  local copies, waits for them, and re-layouts: 21.7 us -> 45.1 us
    all_gather x2 -> x0, waiting for transfers between devices: 52 us -> none  [gathered_inner(): lax.all_gather(local_trial, 'pts', axis=2, tiled=True)]
    all_to_all x0 -> x2, blocking collectives: none -> 38.2 us  [raise_sites(): return jax.lax.all_to_all(response, which_axis, 2, 2, tiled=True)]
    unnamed x22 -> x33, local copies, waits for them, and re-layouts: 15.6 us -> 31.7 us
    concatenate x0 -> x4, local copies, waits for them, and re-layouts: none -> 7.26 us  [raise_sites(): response = jnp.concatenate([arr_in] * jax.lax.axis_size(which_axis), 2)]
    unnamed x12 -> x10, waiting for transfers between devices: 143 us -> 142 us
  transfers between devices with their start and end apart: 8 -> 6, of which waited for: 8 -> 6; matrix products, arithmetic and copies ran while one was open for 1% -> 1% of each run, Pallas kernels for 0% -> 0%
where the time goes in v1:
time: 333 us; the launch traced here: 332 us
  waiting for transfers between devices  185 us (56%)
  blocking collectives  62.1 us (19%)
  local copies, waits for them, and re-layouts  45.1 us (14%)
  matrix products  22.7 us (7%)
  between operations  14.3 us (4%)
    unnamed x10, waiting for transfers between devices  142 us
    reduce_scatter x2, waiting for transfers between devices, orbital_terms(): lax.psum_scatter(rho_part, 'val', scatter_dimension=1, tiled=True)  42.3 us
    all_to_all x2, blocking collectives, raise_sites(): return jax.lax.all_to_all(response, which_axis, 2, 2, tiled=True)  38.2 us
    unnamed x33, local copies, waits for them, and re-layouts  31.7 us
    psum x2, blocking collectives, orbital_terms(): image = lax.psum(image_rows, 'val')  23.9 us
    dot_general x2, matrix products, orbital_terms(): jnp.einsum('km,nm->kn', rho, kernel, preferred_element_type=jnp.float32)  7.52 us
    concatenate x4, local copies, waits for them, and re-layouts, raise_sites(): response = jnp.concatenate([arr_in] * jax.lax.axis_size(which_axis), 2)  7.26 us
    dot_general x2, matrix products, orbital_terms(): rho_part = jnp.einsum('mv,kvm->km', psi_val.astype(jnp.float32), inner)  6.81 us
  transfers between devices with their start and end apart: 6, of which 6 were waited for; matrix products, arithmetic and copies ran while one was open for 1% of the time, Pallas kernels for 0%

profile of v1, /device:TPU:0, one launch (start us, length us, event | category | flops | bytes accessed | tf_op | source)
XLA Modules:
  0.0 331.8 jit_solution(13152471250227471124)
XLA Ops:
  7.2 1.7 constant_dynamic-update-slice_fusion.7
  8.9 1.6 constant_dynamic-update-slice_fusion.6
  10.5 1.6 constant_dynamic-update-slice_fusion.5
  12.1 1.6 constant_dynamic-update-slice_fusion.4
  13.7 1.6 constant_dynamic-update-slice_fusion.3
  15.3 1.6 constant_dynamic-update-slice_fusion.2
  16.9 1.6 constant_dynamic-update-slice_fusion.1
  18.5 1.6 constant_dynamic-update-slice_fusion
  20.1 2.5 copy.20
  22.6 20.3 %all_to_all.10 = bf16[2,256,1024]{1,0,2:T(2,128)(2,1)S(1)} all-to-all(bf16[2,256,1024]{1,0,2:T(2,128)(2,1)S(1)} %copy.20), channel_id=1, replica_groups=mesh['pts'=8,'val'=4] {'pts'}, dimensions={2} | all-to-all | bytes 2097152 | tf_op jit(solution)/shard_map/all_to_all | solution.py:14
  42.9 1.3 fusion.6
  44.2 2.0 copy.24
  46.3 3.4 %fusion.22 = f32[1024,1,2]{2,1,0:T(1,128)} fusion(bf16[2,256,1024]{1,0,2:T(2,128)(2,1)} %copy.24, bf16[1024,256,1]{1,0,2:T(8,128)(2,1)} %bitcast.46), kind=kOutput, calls=%fused_computation.23 | convolution fusion | flops 1048576 | bytes 1581056 | tf_op jit(solution)/shard_map/mv,kvm->km/dot_general | solution.py:25
  49.7 21.3 %reduce-scatter.15.cloned.1.call-done = f32[2,256]{0,1:T(8,128)} async-done(((f32[2,1024]{0,1:T(8,128)}), f32[2,256]{0,1:T(8,128)}) %reduce-scatter.15.cloned.1.call-update) | async-done | bytes 2064 | tf_op jit(solution)/shard_map/reduce_scatter | solution.py:26
  71.1 3.4 %convolution_convert_fusion.1 = bf16[2,8192]{1,0:T(2,128)(2,1)S(1)} fusion(bf16[8192,256]{1,0:T(8,128)(2,1)} %param.9, f32[2,256]{0,1:T(8,128)} %reduce-scatter.15.cloned.1.call-done), kind=kOutput, calls=%fused_computation.1 | convolution fusion | flops 8405504 | bytes 4229120 | tf_op jit(solution)/shard_map/km,nm->kn/dot_general | solution.py:27
  74.5 1.9 copy.29
  76.5 1.1 convert_bitcast_fusion
  77.6 1.3 copy.19
  78.9 37.0 %reduce-scatter.19.cloned.1.call-done = bf16[1024,2]{1,0:T(8,128)(2,1)} async-done(((bf16[8192,2]{1,0:T(8,128)(2,1)}), bf16[1024,2]{1,0:T(8,128)(2,1)}) %reduce-scatter.19.cloned.1.call-update) | async-done | bytes 4112
  115.9 1.1 copy.30
  117.0 11.9 %psum.14 = f32[2,1024]{1,0:T(2,128)S(1)} all-reduce(bf16[2,1024]{1,0:T(2,128)(2,1)S(1)} %copy.30), channel_id=1, replica_groups=mesh['pts'=8,'val'=4] {'val'}, use_global_device_ids=true, to_apply=%region_2.0 | all-reduce | flops 2048 | bytes 12288 | tf_op jit(solution)/shard_map/psum | solution.py:31
  128.9 3.5 %fusion.8 = bf16[2,256,1024]{2,1,0:T(8,128)(2,1)} fusion(bf16[1024,1024]{1,0:T(8,128)(2,1)S(1)} %copy-done, f32[2,1024]{1,0:T(2,128)S(1)} %psum.14, f32[256,1024]{1,0:T(8,128)} %copy.19), kind=kOutput, calls=%fused_computation.12 | convolution fusion | flops 1075314688 | bytes 4202496 | tf_op jit(solution)/shard_map/kvm,mc->kvc/dot_general | solution.py:35
  132.4 2.5 copy.31
  134.9 1.2 copy.37
  136.2 0.8 dynamic-slice.4
  137.1 32.4 %reduce-scatter.21.cloned.1.call-done = bf16[128,512]{1,0:T(8,128)(2,1)} async-done(((bf16[1024,512]{1,0:T(8,128)(2,1)}), bf16[128,512]{1,0:T(8,128)(2,1)}) %reduce-scatter.21.cloned.1.call-update) | async-done | bytes 131088
  169.5 0.9 reshape.18
  170.6 0.8 constant_dynamic-update-slice_fusion.15
  171.4 0.7 constant_dynamic-update-slice_fusion.14
  172.1 0.7 constant_dynamic-update-slice_fusion.13
  174.1 0.7 constant_dynamic-update-slice_fusion.10
  176.2 2.5 copy.22
  178.7 17.9 %all_to_all.11 = bf16[2,256,1024]{1,0,2:T(2,128)(2,1)S(1)} all-to-all(bf16[2,256,1024]{1,0,2:T(2,128)(2,1)S(1)} %copy.22), channel_id=1, replica_groups=mesh['pts'=8,'val'=4] {'pts'}, dimensions={2} | all-to-all | bytes 2097152 | tf_op jit(solution)/shard_map/all_to_all | solution.py:14
  196.6 1.3 fusion.2
  197.9 2.0 copy.27
  200.0 3.4 %fusion.20 = f32[1024,1,2]{2,1,0:T(1,128)} fusion(bf16[2,256,1024]{1,0,2:T(2,128)(2,1)} %copy.27, bf16[1024,256,1]{1,0,2:T(8,128)(2,1)} %bitcast.47), kind=kOutput, calls=%fused_computation.21 | convolution fusion | flops 1048576 | bytes 1581056 | tf_op jit(solution)/shard_map/mv,kvm->km/dot_general | solution.py:25
  203.4 21.0 %reduce-scatter.17.cloned.1.call-done = f32[2,256]{0,1:T(8,128)} async-done(((f32[2,1024]{0,1:T(8,128)}), f32[2,256]{0,1:T(8,128)}) %reduce-scatter.17.cloned.1.call-update) | async-done | bytes 2064 | tf_op jit(solution)/shard_map/reduce_scatter | solution.py:26
  224.5 4.1 %convolution_convert_fusion = bf16[2,8192]{1,0:T(2,128)(2,1)} fusion(bf16[8192,256]{1,0:T(8,128)(2,1)} %param.9, f32[2,256]{0,1:T(8,128)} %reduce-scatter.17.cloned.1.call-done), kind=kOutput, calls=%fused_computation | convolution fusion | flops 8405504 | bytes 4229120 | tf_op jit(solution)/shard_map/km,nm->kn/dot_general | solution.py:27
  228.6 2.7 copy.33
  231.3 39.4 %reduce-scatter.23.cloned.1.call-done = bf16[1024,2]{1,0:T(8,128)(2,1)} async-done(((bf16[8192,2]{1,0:T(8,128)(2,1)}), bf16[1024,2]{1,0:T(8,128)(2,1)}) %reduce-scatter.23.cloned.1.call-update) | async-done | bytes 4112
  270.7 1.1 copy.34
  271.8 11.9 %psum.15 = f32[2,1024]{1,0:T(2,128)S(1)} all-reduce(bf16[2,1024]{1,0:T(2,128)(2,1)S(1)} %copy.34), channel_id=1, replica_groups=mesh['pts'=8,'val'=4] {'val'}, use_global_device_ids=true, to_apply=%region_6.0 | all-reduce | flops 2048 | bytes 12288 | tf_op jit(solution)/shard_map/psum | solution.py:31
  283.7 2.2 fusion.11
  286.0 2.5 copy.35
  288.5 1.2 copy.38
  289.7 33.3 %reduce-scatter.25.cloned.1.call-done = bf16[128,512]{1,0:T(8,128)(2,1)} async-done(((bf16[1024,512]{1,0:T(8,128)(2,1)}), bf16[128,512]{1,0:T(8,128)(2,1)}) %reduce-scatter.25.cloned.1.call-update) | async-done | bytes 131088
  323.1 0.9 reshape.22
  324.2 0.8 convert_subtract_fusion
  (27 shorter events, 3.4 us)
Async XLA Ops:
  7.2 35.7 %copy-start = (bf16[1024,1024]{1,0:T(8,128)(2,1)S(1)}, bf16[1024,1024]{1,0:T(8,128)(2,1)}, u32[]{:S(2)}) copy-start(bf16[1024,1024]{1,0:T(8,128)(2,1)} %param.8) | copy-start | bytes 6291460
  7.2 63.9 %reduce-scatter.15.cloned.1.call-start = ((), (), s32[]{:S(2)}) async-start(), calls=%async_computation.8 | async-start | bytes 655360 | tf_op jit(solution)/shard_map/reduce_scatter | solution.py:26
  49.7 66.2 %reduce-scatter.19.cloned.1.call-start = ((), (), s32[]{:S(2)}) async-start(), calls=%async_computation.10 | async-start | bytes 2359296
  76.4 93.1 %reduce-scatter.21.cloned.1.call-start = ((), (), s32[]{:S(2)}) async-start(), calls=%async_computation.11 | async-start | bytes 1179648
  134.9 2.1 copy-start.3
  134.9 35.7 %copy-start.1 = (bf16[2,256,128]{2,1,0:T(8,128)(2,1)S(1)}, bf16[2,256,128]{2,1,0:T(8,128)(2,1)}, u32[]{:S(2)}) copy-start(bf16[2,256,128]{2,1,0:T(8,128)(2,1)} %param.6) | copy-start | bytes 393220
  136.1 88.3 %reduce-scatter.17.cloned.1.call-start = ((), (), s32[]{:S(2)}) async-start(), calls=%async_computation.9 | async-start | bytes 655360 | tf_op jit(solution)/shard_map/reduce_scatter | solution.py:26
  203.4 67.3 %reduce-scatter.23.cloned.1.call-start = ((), (), s32[]{:S(2)}) async-start(), calls=%async_computation.12 | async-start | bytes 2359296
  228.6 55.2 %copy-start.2 = (f32[256,1024]{1,0:T(8,128)S(1)}, f32[256,1024]{1,0:T(8,128)}, u32[]{:S(2)}) copy-start(f32[256,1024]{1,0:T(8,128)} %copy.19) | copy-start | bytes 3145732
  231.3 91.8 %reduce-scatter.25.cloned.1.call-start = ((), (), s32[]{:S(2)}) async-start(), calls=%async_computation.13 | async-start | bytes 1179648
Sparse Core Ops, SparseCore 0:
  49.8 21.1 reduce-scatter.14
  76.6 39.2 reduce-scatter.18
  136.3 33.1 reduce-scatter.20
  203.5 20.9 reduce-scatter.16
  231.4 39.2 reduce-scatter.22
  289.9 33.1 reduce-scatter.24
